TPU v7x, 128 devices: a whole 4x4x4 slice. The times are simulated.
128 devices in a mesh: dp: 8 (over x, y_lo), tensor: 16 (over y_hi, z, core).
Axes of the slice: x: 4, y: 4 (y_hi: 2, y_lo: 2; y = y_hi * 2 + y_lo), z: 4, core: 2. Of those that a mesh axis runs over, the one named last changes fastest.
Arguments:
- enc_tokens: bfloat16 [128, 128, 1024], P(('dp', 'tensor')), may hold values from -6 to 6
- src_lengths: int32 [128], replicated, may hold values from 1 to 128, as said below
- enc_gain: float32 [1024], replicated, may hold values from 0.1 to 1.9
- enc_query: bfloat16 [1024, 8192], P(None, 'tensor'), may hold values from -0.1875 to 0.1875
- enc_key: bfloat16 [1024, 8192], P(None, 'tensor'), may hold values from -0.1875 to 0.1875
- enc_value: bfloat16 [1024, 8192], P(None, 'tensor'), may hold values from -0.1875 to 0.1875
- enc_output: bfloat16 [8192, 1024], P('tensor'), may hold values from -0.0625 to 0.0625
- enc_bias: float32 [64, 33], P('tensor'), may hold values from -3 to 260
- mem_gain: float32 [1024], replicated, may hold values from 0.1 to 1.9
- dec_tokens: bfloat16 [128, 64, 1024], P(('dp', 'tensor')), may hold values from -6 to 6
- tgt_lengths: int32 [128], P(('dp', 'tensor')), may hold values from 1 to 64
- lang_tags: int32 [128], P('dp'), may hold values from 0 to 7
- lang_table: bfloat16 [8, 1024], replicated, may hold values from -6 to 6
- cross_gain: float32 [1024], replicated, may hold values from 0.1 to 1.9
- cross_query: bfloat16 [1024, 8192], P(None, 'tensor'), may hold values from -0.1875 to 0.1875
- cross_key: bfloat16 [1024, 8192], P(None, 'tensor'), may hold values from -0.1875 to 0.1875
- cross_value: bfloat16 [1024, 8192], P(None, 'tensor'), may hold values from -0.1875 to 0.1875
- cross_output: bfloat16 [8192, 1024], P('tensor'), may hold values from -0.0625 to 0.0625
- ffn_gain: float32 [1024], replicated, may hold values from 0.1 to 1.9
- ffn_in: bfloat16 [1024, 32768], P(None, 'tensor'), may hold values from -0.1875 to 0.1875
- ffn_out: bfloat16 [32768, 1024], P('tensor'), may hold values from -0.03125 to 0.03125
Outputs:
- enc_memory: bfloat16 [128, 128, 1024], P(('dp', 'tensor'))
- dec_out: bfloat16 [128, 64, 1024], P(('dp', 'tensor'))
Inputs may be any that keep to these rules, and one draw needn't show every extreme that they name: `src_lengths`: never falling along the batch; the first is 1 and the last is 128.
All inputs are finite; a program needn't handle non-finite values.
Results may differ from a plain program's by a relative error of at most 0.014.
Values may be sent and summed in bfloat16 or wider, within the bound.
A program may use at most 128 MiB of HBM per device.

v0:
```python
import jax
import jax.numpy as jnp
from jax import lax
from jax.sharding import PartitionSpec as P

HD = 128
MAXREL = 16
NB = 33
EPSILON = 1e-06
NEG_FILL = -1e30


def rms_norm(values, norm_gain):
    mean_sq = jnp.mean(values * values, axis=-1, keepdims=True)
    return values * lax.rsqrt(mean_sq + EPSILON) * norm_gain


def make_grid(bias_table, query_len, key_len):
    offset = jnp.arange(key_len)[None, :] - jnp.arange(query_len)[:, None]
    bucket = (jnp.clip(offset, -MAXREL, MAXREL) + MAXREL).reshape(1, query_len * key_len)
    onehot = (bucket == jnp.arange(NB)[:, None]).astype(jnp.float32)
    flat_grid = jnp.dot(
        bias_table, onehot, precision=lax.Precision.HIGHEST, preferred_element_type=jnp.float32
    )
    return flat_grid.reshape(bias_table.shape[0], query_len, key_len)


def attend(query_rows, key_rows, value_rows, bias_table, lengths):
    examples, query_len, columns = query_rows.shape
    key_len = key_rows.shape[1]
    head_count = columns // HD
    query_heads = query_rows.reshape(examples, query_len, head_count, HD)
    key_heads = key_rows.reshape(examples, key_len, head_count, HD)
    value_heads = value_rows.reshape(examples, key_len, head_count, HD)
    scores = jnp.einsum(
        "eqhd,ekhd->ehqk", query_heads, key_heads, preferred_element_type=jnp.float32
    )
    scores = scores * HD ** (-0.5)
    if bias_table is not None:
        scores = scores + make_grid(bias_table, query_len, key_len)[None]
    key_valid = jnp.arange(key_len)[None, :] < lengths[:, None]
    scores = jnp.where(key_valid[:, None, None, :], scores, NEG_FILL)
    row_max = jnp.max(scores, axis=-1, keepdims=True)
    exponent = jnp.exp(scores - row_max)
    weights = (exponent / jnp.sum(exponent, axis=-1, keepdims=True)).astype(jnp.bfloat16)
    context = jnp.einsum(
        "ehqk,ekhd->eqhd", weights, value_heads, preferred_element_type=jnp.float32
    )
    return context.astype(jnp.bfloat16).reshape(examples, query_len, columns)


def widen(values):
    return lax.all_gather(values, "tensor", axis=0, tiled=True)


def narrow(partial_value):
    return lax.psum_scatter(
        partial_value.astype(jnp.bfloat16), "tensor", scatter_dimension=0, tiled=True
    ).astype(jnp.float32)


def restripe(values):
    groups = lax.axis_size("dp")
    per_pair = values.shape[0] // groups
    shaped = values.reshape((per_pair, groups) + values.shape[1:])
    arrived = lax.all_to_all(shaped, "dp", split_axis=1, concat_axis=0, tiled=True)
    return arrived.reshape(values.shape)


def project(rows, weight):
    flat_rows = rows.reshape(-1, rows.shape[-1])
    result = jnp.dot(flat_rows, weight, preferred_element_type=jnp.float32).astype(jnp.bfloat16)
    return result.reshape(rows.shape[:-1] + (weight.shape[1],))


def output_terms(context, weight):
    flat_rows = context.reshape(-1, context.shape[-1])
    result = jnp.dot(flat_rows, weight, preferred_element_type=jnp.float32)
    return result.reshape(context.shape[:-1] + (weight.shape[1],))


def on_device(
    enc_tokens,
    src_lengths,
    enc_gain,
    enc_query,
    enc_key,
    enc_value,
    enc_output,
    enc_bias,
    mem_gain,
    dec_tokens,
    tgt_lengths,
    lang_tags,
    lang_table,
    cross_gain,
    cross_query,
    cross_key,
    cross_value,
    cross_output,
    ffn_gain,
    ffn_in,
    ffn_out,
):
    groups = lax.axis_size("dp")
    group_index = lax.axis_index("dp")
    tensor_index = lax.axis_index("tensor")
    local_ex = enc_tokens.shape[0]
    examples = local_ex * lax.axis_size("tensor")
    per_pair = examples // groups
    enc_len = lax.dynamic_slice_in_dim(src_lengths, group_index * examples, examples)
    dec_src_len = lax.dynamic_index_in_dim(
        src_lengths.reshape(groups, per_pair, groups), group_index, axis=2, keepdims=False
    ).reshape(examples)
    enc_input = enc_tokens.astype(jnp.float32)
    enc_normed = rms_norm(enc_input, enc_gain).astype(jnp.bfloat16)
    enc_rows = widen(enc_normed)
    enc_context = attend(
        project(enc_rows, enc_query),
        project(enc_rows, enc_key),
        project(enc_rows, enc_value),
        enc_bias,
        enc_len,
    )
    enc_hidden = enc_input + narrow(output_terms(enc_context, enc_output))
    enc_memory = rms_norm(enc_hidden, mem_gain).astype(jnp.bfloat16)
    dec_memory = restripe(widen(enc_memory))
    cross_k = project(dec_memory, cross_key)
    cross_v = project(dec_memory, cross_value)
    lang_onehot = (lang_tags[:, None] == jnp.arange(lang_table.shape[0])[None, :]).astype(
        jnp.bfloat16
    )
    lang_rows = jnp.dot(lang_onehot, lang_table, preferred_element_type=jnp.float32)[:, None, :]
    dec_full = widen(dec_tokens).astype(jnp.float32) + lang_rows
    dec_normed = rms_norm(dec_full, cross_gain).astype(jnp.bfloat16)
    cross_context = attend(project(dec_normed, cross_query), cross_k, cross_v, None, dec_src_len)
    cross_terms = output_terms(cross_context, cross_output)
    local_lang = lax.dynamic_slice_in_dim(lang_rows, tensor_index * local_ex, local_ex, 0)
    hidden_local = dec_tokens.astype(jnp.float32) + local_lang + narrow(cross_terms)
    ffn_rows = widen(rms_norm(hidden_local, ffn_gain).astype(jnp.bfloat16))
    flat_rows = ffn_rows.reshape(-1, ffn_rows.shape[-1])
    activated = jnp.maximum(
        jnp.dot(flat_rows, ffn_in, preferred_element_type=jnp.float32), 0.0
    ).astype(jnp.bfloat16)
    activated = activated.reshape(ffn_rows.shape[:-1] + (ffn_in.shape[1],))
    dec_sum = hidden_local + narrow(output_terms(activated, ffn_out))
    target_len = dec_tokens.shape[1]
    keep = jnp.arange(target_len)[None, :] < tgt_lengths[:, None]
    dec_out = jnp.where(keep[:, :, None], dec_sum, 0.0).astype(jnp.bfloat16)
    return (enc_memory, dec_out)


def solution(mesh):
    in_specs = (
        P(("dp", "tensor"), None, None),
        P(),
        P(),
        P(None, "tensor"),
        P(None, "tensor"),
        P(None, "tensor"),
        P("tensor", None),
        P("tensor", None),
        P(),
        P(("dp", "tensor"), None, None),
        P(("dp", "tensor")),
        P("dp"),
        P(),
        P(),
        P(None, "tensor"),
        P(None, "tensor"),
        P(None, "tensor"),
        P("tensor", None),
        P(),
        P(None, "tensor"),
        P("tensor", None),
    )
    out_specs = (P(("dp", "tensor"), None, None), P(("dp", "tensor"), None, None))
    return jax.shard_map(
        on_device, mesh=mesh, in_specs=in_specs, out_specs=out_specs, check_vma=False
    )
```

profile of v0, /device:TPU:0, one launch (start us, length us, event | category | flops | bytes accessed | tf_op | source)
XLA Modules:
  0.0 565.8 jit_solution(7086477349250466452)
XLA Ops:
  8.5 1.8 fusion.41
  10.4 1.7 fusion.29
  12.4 56.7 %all-gather.5.cloned.1.call-done = bf16[16,128,1024]{2,1,0:T(8,128)(2,1)} async-done(((bf16[1,128,1024]{2,1,0:T(8,128)(2,1)}), bf16[16,128,1024]{2,1,0:T(8,128)(2,1)}) %all-gather.5.cloned.1.call-update) | async-done | bytes 4194320 | tf_op jit(solution)/shard_map/all_gather | solution.py:53
  69.0 5.9 %convolution_convert_fusion.2 = bf16[2048,512]{1,0:T(8,128)(2,1)} fusion(bf16[2048,1024]{1,0:T(8,128)(2,1)} %bitcast.61, bf16[1024,512]{1,0:T(8,128)(2,1)S(1)} %copy-done.16), kind=kOutput, calls=%fused_computation.11 | convolution fusion | flops 2148532224 | bytes 7340032 | tf_op jit(solution)/shard_map/dot_general | solution.py:72
  74.9 2.5 reshape_reshape.26
  77.5 6.3 %convolution_convert_fusion.3 = bf16[2048,512]{1,0:T(8,128)(2,1)} fusion(bf16[2048,1024]{1,0:T(8,128)(2,1)} %bitcast.62, bf16[1024,512]{1,0:T(8,128)(2,1)} %param.24), kind=kOutput, calls=%fused_computation.12 | convolution fusion | flops 2148532224 | bytes 7340032 | tf_op jit(solution)/shard_map/dot_general | solution.py:72
  83.8 3.7 convolution_convert_fusion.4
  87.5 4.0 reshape_reshape.24
  91.4 4.0 reshape_reshape.25
  95.4 3.2 fusion.10
  98.6 1.8 fusion.54
  101.3 4.3 convolution_convert_fusion.5
  105.7 78.5 %reduce-scatter.4.cloned.1.call-done = bf16[1,128,1024]{2,1,0:T(8,128)(2,1)} async-done(((bf16[16,128,1024]{2,1,0:T(8,128)(2,1)}), bf16[1,128,1024]{2,1,0:T(8,128)(2,1)}) %reduce-scatter.4.cloned.1.call-update) | async-done | bytes 262160 | tf_op jit(solution)/shard_map/reduce_scatter | solution.py:57
  185.4 1.8 multiply_convert_fusion.1
  187.7 54.1 %all-gather.7.cloned.1.call-done = bf16[16,128,1024]{2,1,0:T(8,128)(2,1)} async-done(((bf16[1,128,1024]{2,1,0:T(8,128)(2,1)}), bf16[16,128,1024]{2,1,0:T(8,128)(2,1)}) %all-gather.7.cloned.1.call-update) | async-done | bytes 4194320 | tf_op jit(solution)/shard_map/all_gather | solution.py:53
  241.8 4.8 copy.70
  246.6 4.7 all-to-all-start
  252.3 60.9 %all-gather.9.cloned.1.call-done = bf16[16,64,1024]{2,1,0:T(8,128)(2,1)} async-done(((bf16[1,64,1024]{2,1,0:T(8,128)(2,1)}), bf16[16,64,1024]{2,1,0:T(8,128)(2,1)}) %all-gather.9.cloned.1.call-update) | async-done | bytes 2097168 | tf_op jit(solution)/shard_map/all_gather | solution.py:53
  313.2 2.4 multiply_reduce_fusion
  319.3 5.9 %convolution_convert_fusion = bf16[2048,512]{1,0:T(8,128)(2,1)} fusion(bf16[2048,1024]{1,0:T(8,128)(2,1)} %bitcast.11, bf16[1024,512]{1,0:T(8,128)(2,1)S(1)} %copy-done.19), kind=kOutput, calls=%fused_computation.9 | convolution fusion | flops 2148532224 | bytes 7340032 | tf_op jit(solution)/shard_map/dot_general | solution.py:72
  325.3 4.5 convolution_convert_fusion.1
  329.8 2.1 reshape_reshape.28
  331.9 2.5 reshape_reshape.30
  334.4 1.5 fusion.7
  338.9 9.8 %fusion.25 = bf16[16,4,8,8,128]{4,3,2,1,0:T(8,128)(2,1)} fusion(bf16[16,128,4,128]{3,2,1,0:T(4,128)(2,1)S(1)} %copy-done.6, f32[16,4,64]{2,1,0:T(4,128)S(1)} %fusion.55, f32[16,4,64,128]{3,2,1,0:T(8,128)} %copy-done.7, pred[16,128]{1,0:T(8,128)(4,1)S(1)} %iota_compare_fusion.4), kind=kOutput, calls=%fused_computation.41 | convolution fusion | flops 137367680 | bytes 5261312 | tf_op jit(solution)/shard_map/ehqk,ekhd->eqhd/dot_general | solution.py:46
  348.7 3.8 convolution_convert_fusion.7
  352.7 70.8 %reduce-scatter.6.cloned.1.call-done = bf16[1,64,1024]{2,1,0:T(8,128)(2,1)} async-done(((bf16[16,64,1024]{2,1,0:T(8,128)(2,1)}), bf16[1,64,1024]{2,1,0:T(8,128)(2,1)}) %reduce-scatter.6.cloned.1.call-update) | async-done | bytes 131088 | tf_op jit(solution)/shard_map/reduce_scatter | solution.py:57
  424.6 1.7 multiply_convert_fusion.2
  426.6 46.4 %all-gather.11.cloned.1.call-done = bf16[16,64,1024]{2,1,0:T(8,128)(2,1)} async-done(((bf16[1,64,1024]{2,1,0:T(8,128)(2,1)}), bf16[16,64,1024]{2,1,0:T(8,128)(2,1)}) %all-gather.11.cloned.1.call-update) | async-done | bytes 2097168 | tf_op jit(solution)/shard_map/all_gather | solution.py:53
  473.0 14.3 %convolution_convert_fusion.6 = bf16[1024,1024]{1,0:T(8,128)(2,1)} fusion(bf16[2048,1024]{1,0:T(8,128)(2,1)} %param.41, bf16[1024,1024]{1,0:T(8,128)(2,1)} %bitcast.64, bf16[1024,2048]{1,0:T(8,128)(2,1)} %param.40), kind=kOutput, calls=%fused_computation.36 | convolution fusion | flops 8595177472 | bytes 12582912 | tf_op jit(solution)/shard_map/dot_general | solution.py:78
  488.0 69.2 %reduce-scatter.8.cloned.1.call-done = bf16[1,64,1024]{2,1,0:T(8,128)(2,1)} async-done(((bf16[16,64,1024]{2,1,0:T(8,128)(2,1)}), bf16[1,64,1024]{2,1,0:T(8,128)(2,1)}) %reduce-scatter.8.cloned.1.call-update) | async-done | bytes 131088 | tf_op jit(solution)/shard_map/reduce_scatter | solution.py:57
  557.3 1.6 select_convert_fusion
  (83 shorter events, 13.5 us)
Async XLA Ops:
  7.2 94.2 %copy-start = (bf16[512,1024]{1,0:T(8,128)(2,1)S(1)}, bf16[512,1024]{1,0:T(8,128)(2,1)}, u32[]{:S(2)}) copy-start(bf16[512,1024]{1,0:T(8,128)(2,1)} %param.27) | copy-start | bytes 3145732
  7.2 5.0 copy-start.14
  7.2 61.8 %copy-start.16 = (bf16[1024,512]{1,0:T(8,128)(2,1)S(1)}, bf16[1024,512]{1,0:T(8,128)(2,1)}, u32[]{:S(2)}) copy-start(bf16[1024,512]{1,0:T(8,128)(2,1)} %param.25) | copy-start | bytes 3145732
  7.2 61.8 %all-gather.5.cloned.1.call-start = ((), (), s32[]{:S(2)}) async-start(), calls=%async_computation.4 | async-start | bytes 4456448 | tf_op jit(solution)/shard_map/all_gather | solution.py:53
  10.3 173.9 %reduce-scatter.4.cloned.1.call-start = ((), (), s32[]{:S(2)}) async-start(), calls=%async_computation.5 | async-start | bytes 4456448 | tf_op jit(solution)/shard_map/reduce_scatter | solution.py:57
  77.4 6.3 %copy-start.15 = (bf16[16,128,1024]{2,1,0:T(8,128)(2,1)S(1)}, bf16[16,128,1024]{2,1,0:T(8,128)(2,1)}, u32[]{:S(2)}) copy-start(bf16[16,128,1024]{2,1,0:T(8,128)(2,1)} %all-gather.5.cloned.1.call-done) | copy-start | bytes 12582916
  77.4 6.3 %copy-start.17 = (bf16[1024,512]{1,0:T(8,128)(2,1)S(1)}, bf16[1024,512]{1,0:T(8,128)(2,1)}, u32[]{:S(2)}) copy-start(bf16[1024,512]{1,0:T(8,128)(2,1)} %param.26) | copy-start | bytes 3145732
  98.5 1.8 copy-start.5
  105.7 78.6 %copy-start.3 = (bf16[1,128,1024]{2,1,0:T(8,128)(2,1)S(1)}, bf16[1,128,1024]{2,1,0:T(8,128)(2,1)}, u32[]{:S(2)}) copy-start(bf16[1,128,1024]{2,1,0:T(8,128)(2,1)} %param.21) | copy-start | bytes 786436
  105.7 79.7 %copy-start.10 = (f32[1024]{0:T(1024)S(1)}, f32[1024]{0:T(1024)}, u32[]{:S(2)}) copy-start(f32[1024]{0:T(1024)} %param.29) | copy-start | bytes 12292
  105.7 136.1 %all-gather.7.cloned.1.call-start = ((), (), s32[]{:S(2)}) async-start(), calls=%async_computation.6 | async-start | bytes 4456448 | tf_op jit(solution)/shard_map/all_gather | solution.py:53
  187.2 126.1 %all-gather.9.cloned.1.call-start = ((), (), s32[]{:S(2)}) async-start(), calls=%async_computation.7 | async-start | bytes 2228224 | tf_op jit(solution)/shard_map/all_gather | solution.py:53
  246.6 5.5 copy-start.9
  246.6 5.5 copy-start.13
  246.6 71.8 %all-to-all-start = ((bf16[2,8,128,1024]{3,2,0,1:T(8,128)(2,1)}), bf16[2,8,128,1024]{3,2,0,1:T(8,128)(2,1)}, u32[]{:S(2)}, u32[]{:S(2)}) async-start(bf16[2,8,128,1024]{3,2,0,1:T(8,128)(2,1)} %copy.70), calls=%async_computation.1 | async-start | bytes 8388608 | tf_op jit(solution)/shard_map/all_to_all | solution.py:66
  251.3 64.3 %copy-start.11 = (f32[1024]{0:T(1024)S(1)}, f32[1024]{0:T(1024)}, u32[]{:S(2)}) copy-start(f32[1024]{0:T(1024)} %param.34) | copy-start | bytes 12292
  251.3 172.2 %reduce-scatter.6.cloned.1.call-start = ((), (), s32[]{:S(2)}) async-start(), calls=%async_computation.8 | async-start | bytes 2228224 | tf_op jit(solution)/shard_map/reduce_scatter | solution.py:57
  313.2 2.4 copy-start.2
  315.6 1.2 copy-start.18
  318.1 1.2 copy-start.19
  319.3 5.9 %copy-start.20 = (bf16[1024,512]{1,0:T(8,128)(2,1)S(1)}, bf16[1024,512]{1,0:T(8,128)(2,1)}, u32[]{:S(2)}) copy-start(bf16[1024,512]{1,0:T(8,128)(2,1)} %param.37) | copy-start | bytes 3145732
  336.0 1.3 copy-start.7
  337.3 1.6 copy-start.6
  338.9 9.8 %copy-start.21 = (bf16[512,1024]{1,0:T(8,128)(2,1)S(1)}, bf16[512,1024]{1,0:T(8,128)(2,1)}, u32[]{:S(2)}) copy-start(bf16[512,1024]{1,0:T(8,128)(2,1)} %param.38) | copy-start | bytes 3145732
  352.6 71.0 %copy-start.4 = (bf16[1,64,1024]{2,1,0:T(8,128)(2,1)S(1)}, bf16[1,64,1024]{2,1,0:T(8,128)(2,1)}, u32[]{:S(2)}) copy-start(bf16[1,64,1024]{2,1,0:T(8,128)(2,1)} %param.30) | copy-start | bytes 393220
  352.6 72.0 %copy-start.12 = (f32[1024]{0:T(1024)S(1)}, f32[1024]{0:T(1024)}, u32[]{:S(2)}) copy-start(f32[1024]{0:T(1024)} %param.39) | copy-start | bytes 12292
  352.6 120.4 %all-gather.11.cloned.1.call-start = ((), (), s32[]{:S(2)}) async-start(), calls=%async_computation.9 | async-start | bytes 2228224 | tf_op jit(solution)/shard_map/all_gather | solution.py:53
  426.3 131.0 %reduce-scatter.8.cloned.1.call-start = ((), (), s32[]{:S(2)}) async-start(), calls=%async_computation.10 | async-start | bytes 2228224 | tf_op jit(solution)/shard_map/reduce_scatter | solution.py:57
  473.0 85.9 %copy-start.1 = (bf16[512,1024]{1,0:T(8,128)(2,1)S(1)}, bf16[512,1024]{1,0:T(8,128)(2,1)}, u32[]{:S(2)}) copy-start(bf16[512,1024]{1,0:T(8,128)(2,1)} %param.27) | copy-start | bytes 3145732
  487.3 70.0 %copy-start.8 = (bf16[1,64,1024]{2,1,0:T(8,128)(2,1)S(1)}, bf16[1,64,1024]{2,1,0:T(8,128)(2,1)}, u32[]{:S(2)}) copy-start(bf16[1,64,1024]{2,1,0:T(8,128)(2,1)} %reduce-scatter.6.cloned.1.call-done) | copy-start | bytes 393220
Sparse Core Ops, SparseCore 0:
  11.1 57.8 all-gather.4
  105.8 78.3 reduce-scatter.3
  187.6 54.2 all-gather.6
  244.5 68.7 all-gather.8
  352.7 70.7 reduce-scatter.5
  426.4 46.5 all-gather.10
  487.5 69.7 reduce-scatter.7
where the time goes:
time: 567 us; the launch traced here: 566 us
  waiting for transfers between devices  437 us (77%)
  matrix products  67.4 us (12%)
  local copies, waits for them, and re-layouts  24.1 us (4%)
  other arithmetic  16.5 us (3%)
  between operations  15.1 us (3%)
    reduce_scatter x3, waiting for transfers between devices, narrow(): lax.psum_scatter(partial_value.astype(jnp.bfloat16), 'tensor', scatter_di...  219 us
    all_gather x4, waiting for transfers between devices, widen(): return lax.all_gather(values, 'tensor', axis=0, tiled=True)  218 us
    dot_general x6, matrix products, project(): jnp.dot(flat_rows, weight, preferred_element_type=jnp.float32)  27.6 us
    dot_general x3, matrix products, output_terms(): result = jnp.dot(flat_rows, weight, preferred_element_type=jnp.float32)  22.5 us
  transfers between devices with their start and end apart: 8, of which 7 were waited for; matrix products, arithmetic and copies ran while one was open for 2% of the time, Pallas kernels for 0%

commit v1 on v0

--- a/solution.py
+++ b/solution.py
@@ -50,7 +50,9 @@
 
 
 def widen(values):
-    return lax.all_gather(values, "tensor", axis=0, tiled=True)
+    return jnp.concatenate(
+        lax.all_to_all(jnp.stack([values] * lax.axis_size("tensor")), "tensor", 0, 0), axis=0
+    )
 
 
 def narrow(partial_value):

time: 567 us -> 593 us (1.046)
  blocking collectives: 0 us -> 89.5 us
  waiting for transfers between devices: 437 us -> 360 us
  starting transfers between devices: 5.45 us -> 17.9 us
    all_gather x4 -> x0, waiting for transfers between devices: 218 us -> none  [widen(): return lax.all_gather(values, 'tensor', axis=0, tiled=True)]
    all_to_all x0 -> x2, blocking collectives: none -> 89.5 us  [widen(): lax.all_to_all(jnp.stack([values] * lax.axis_size('tensor')), 'tensor', 0...]
    all_to_all x0 -> x2, waiting for transfers between devices: none -> 78.7 us  [widen(): lax.all_to_all(jnp.stack([values] * lax.axis_size('tensor')), 'tensor', 0...]
    all_to_all x1, waiting for transfers between devices: 0.01 us -> 54.8 us  [restripe(): lax.all_to_all(shaped, 'dp', split_axis=1, concat_axis=0, tiled=True)]
    all_to_all x0 -> x2, starting transfers between devices: none -> 12 us  [widen(): lax.all_to_all(jnp.stack([values] * lax.axis_size('tensor')), 'tensor', 0...]
    another operation x1 -> x6, local copies, waits for them, and re-layouts: 0.01 us -> 9.66 us  [the longest x4 4.93 us: widen(): jnp.stack([values] * lax.axis_size('tensor'))]
    reduce_scatter x3, waiting for transfers between devices: 219 us -> 227 us  [narrow(): lax.psum_scatter(partial_value.astype(jnp.bfloat16), 'tensor', scatter_di...]
  transfers between devices with their start and end apart: 8 -> 6, of which waited for: 7 -> 6; matrix products, arithmetic and copies ran while one was open for 2% -> 2% of each run, Pallas kernels for 0% -> 0%
where the time goes in v1:
time: 593 us; the launch traced here: 592 us
  waiting for transfers between devices  360 us (61%)
  blocking collectives  89.5 us (15%)
  matrix products  68.1 us (11%)
  local copies, waits for them, and re-layouts  28.4 us (5%)
  starting transfers between devices  17.9 us (3%)
  between operations  14.7 us (2%)
  other arithmetic  12.6 us (2%)
    reduce_scatter x3, waiting for transfers between devices, narrow(): lax.psum_scatter(partial_value.astype(jnp.bfloat16), 'tensor', scatter_di...  227 us
    all_to_all x2, blocking collectives, widen(): lax.all_to_all(jnp.stack([values] * lax.axis_size('tensor')), 'tensor', 0...  89.5 us
    all_to_all x2, waiting for transfers between devices, widen(): lax.all_to_all(jnp.stack([values] * lax.axis_size('tensor')), 'tensor', 0...  78.7 us
    all_to_all x1, waiting for transfers between devices, restripe(): lax.all_to_all(shaped, 'dp', split_axis=1, concat_axis=0, tiled=True)  54.8 us
    dot_general x6, matrix products, project(): jnp.dot(flat_rows, weight, preferred_element_type=jnp.float32)  29.7 us
    dot_general x3, matrix products, output_terms(): result = jnp.dot(flat_rows, weight, preferred_element_type=jnp.float32)  21.8 us
    all_to_all x2, starting transfers between devices, widen(): lax.all_to_all(jnp.stack([values] * lax.axis_size('tensor')), 'tensor', 0...  12 us
  transfers between devices with their start and end apart: 6, of which 6 were waited for; matrix products, arithmetic and copies ran while one was open for 2% of the time, Pallas kernels for 0%

profile of v1, /device:TPU:0, one launch (start us, length us, event | category | flops | bytes accessed | tf_op | source)
XLA Modules:
  0.0 591.6 jit_solution(14725179668424665748)
XLA Ops:
  9.5 2.5 stack.8
  12.0 8.3 %all-to-all-start = ((bf16[16,1,128,1024]{3,2,1,0:T(8,128)(2,1)}), bf16[16,1,128,1024]{3,2,1,0:T(8,128)(2,1)}, u32[]{:S(2)}, u32[]{:S(2)}) async-start(bf16[16,1,128,1024]{3,2,1,0:T(8,128)(2,1)} %stack.8), calls=%async_computation | async-start | bytes 8388608 | tf_op jit(solution)/shard_map/all_to_all | solution.py:54
  21.7 54.1 %all-to-all-done = bf16[16,1,128,1024]{3,2,1,0:T(8,128)(2,1)} async-done(((bf16[16,1,128,1024]{3,2,1,0:T(8,128)(2,1)}), bf16[16,1,128,1024]{3,2,1,0:T(8,128)(2,1)}, u32[]{:S(2)}, u32[]{:S(2)}) %all-to-all-start) | async-done | bytes 4194336 | tf_op jit(solution)/shard_map/all_to_all | solution.py:54
  75.8 5.9 convolution_convert_fusion.2
  81.7 2.5 reshape_reshape.38
  84.2 6.2 %convolution_convert_fusion.3 = bf16[2048,512]{1,0:T(8,128)(2,1)} fusion(bf16[2048,1024]{1,0:T(8,128)(2,1)} %bitcast.1, bf16[1024,512]{1,0:T(8,128)(2,1)} %param.24), kind=kOutput, calls=%fused_computation.16 | convolution fusion | flops 2148532224 | bytes 7340032 | tf_op jit(solution)/shard_map/dot_general | solution.py:74
  90.5 5.9 convolution_convert_fusion.4
  96.4 4.0 reshape_reshape.36
  100.3 4.0 reshape_reshape.37
  104.3 3.2 fusion.15
  107.5 1.8 fusion.61
  110.1 4.3 convolution_convert_fusion.5
  114.5 87.8 %reduce-scatter.4.cloned.1.call-done = bf16[1,128,1024]{2,1,0:T(8,128)(2,1)} async-done(((bf16[16,128,1024]{2,1,0:T(8,128)(2,1)}), bf16[1,128,1024]{2,1,0:T(8,128)(2,1)}) %reduce-scatter.4.cloned.1.call-update) | async-done | bytes 262160 | tf_op jit(solution)/shard_map/reduce_scatter | solution.py:59
  205.2 55.8 %all_to_all.35 = bf16[16,1,128,1024]{3,2,1,0:T(8,128)(2,1)} all-to-all(bf16[16,1,128,1024]{3,2,1,0:T(8,128)(2,1)S(1)} %stack.9), channel_id=1, replica_groups=mesh['dp'=8,'tensor'=16] {'tensor'}, dimensions={0} | all-to-all | bytes 8388608 | tf_op jit(solution)/shard_map/all_to_all | solution.py:54
  261.1 1.7 stack.10
  262.7 3.7 all-to-all-start.3
  266.5 4.7 copy.81
  271.2 24.5 %all-to-all-done.3 = bf16[16,1,64,1024]{3,2,1,0:T(8,128)(2,1)S(1)} async-done(((bf16[16,1,64,1024]{3,2,1,0:T(8,128)(2,1)}), bf16[16,1,64,1024]{3,2,1,0:T(8,128)(2,1)S(1)}, u32[]{:S(2)}, u32[]{:S(2)}) %all-to-all-start.3) | async-done | bytes 2097184 | tf_op jit(solution)/shard_map/all_to_all | solution.py:54
  295.7 5.5 all-to-all-start.2
  305.7 54.8 %all-to-all-done.2 = bf16[2,8,128,1024]{3,2,0,1:T(8,128)(2,1)} async-done(((bf16[2,8,128,1024]{3,2,0,1:T(8,128)(2,1)}), bf16[2,8,128,1024]{3,2,0,1:T(8,128)(2,1)}, u32[]{:S(2)}, u32[]{:S(2)}) %all-to-all-start.2) | async-done | bytes 4194336 | tf_op jit(solution)/shard_map/all_to_all | solution.py:68
  360.6 5.9 convolution_convert_fusion
  366.5 4.5 convolution_convert_fusion.1
  371.0 2.1 reshape_reshape.41
  373.1 2.5 reshape_reshape.43
  375.7 1.5 fusion.12
  380.1 9.9 %fusion.30 = bf16[16,4,8,8,128]{4,3,2,1,0:T(8,128)(2,1)} fusion(bf16[16,128,4,128]{3,2,1,0:T(4,128)(2,1)S(1)} %copy-done.5, f32[16,4,64]{2,1,0:T(4,128)S(1)} %fusion.62, f32[16,4,64,128]{3,2,1,0:T(8,128)} %copy-done.6, pred[16,128]{1,0:T(8,128)(4,1)S(1)} %iota_compare_fusion.4), kind=kOutput, calls=%fused_computation.45 | convolution fusion | flops 137367680 | bytes 5261312 | tf_op jit(solution)/shard_map/ehqk,ekhd->eqhd/dot_general | solution.py:46
  390.0 3.8 convolution_convert_fusion.7
  393.9 71.4 %reduce-scatter.6.cloned.1.call-done = bf16[1,64,1024]{2,1,0:T(8,128)(2,1)} async-done(((bf16[16,64,1024]{2,1,0:T(8,128)(2,1)}), bf16[1,64,1024]{2,1,0:T(8,128)(2,1)}) %reduce-scatter.6.cloned.1.call-update) | async-done | bytes 131088 | tf_op jit(solution)/shard_map/reduce_scatter | solution.py:59
  467.6 33.7 %all_to_all.36 = bf16[16,1,64,1024]{3,2,1,0:T(8,128)(2,1)S(1)} all-to-all(bf16[16,1,64,1024]{3,2,1,0:T(8,128)(2,1)S(1)} %stack.11), channel_id=1, replica_groups=mesh['dp'=8,'tensor'=16] {'tensor'}, dimensions={0} | all-to-all | bytes 4194304 | tf_op jit(solution)/shard_map/all_to_all | solution.py:54
  501.3 13.7 %convolution_convert_fusion.6 = bf16[1024,1024]{1,0:T(8,128)(2,1)} fusion(bf16[2048,1024]{1,0:T(8,128)(2,1)} %param.41, bf16[1024,1024]{1,0:T(8,128)(2,1)S(1)} %bitcast.78, bf16[1024,2048]{1,0:T(8,128)(2,1)} %param.40), kind=kOutput, calls=%fused_computation.40 | convolution fusion | flops 8595177472 | bytes 12582912 | tf_op jit(solution)/shard_map/dot_general | solution.py:80
  515.7 67.7 %reduce-scatter.8.cloned.1.call-done = bf16[1,64,1024]{2,1,0:T(8,128)(2,1)} async-done(((bf16[16,64,1024]{2,1,0:T(8,128)(2,1)}), bf16[1,64,1024]{2,1,0:T(8,128)(2,1)}) %reduce-scatter.8.cloned.1.call-update) | async-done | bytes 131088 | tf_op jit(solution)/shard_map/reduce_scatter | solution.py:59
  583.4 1.6 select_convert_fusion
  (82 shorter events, 17.2 us)
Async XLA Ops:
  7.2 103.0 %copy-start = (bf16[512,1024]{1,0:T(8,128)(2,1)S(1)}, bf16[512,1024]{1,0:T(8,128)(2,1)}, u32[]{:S(2)}) copy-start(bf16[512,1024]{1,0:T(8,128)(2,1)} %param.27) | copy-start | bytes 3145732
  12.0 8.4 %copy-start.21 = (f32[4,33]{1,0:T(4,128)S(1)}, f32[4,33]{1,0:T(4,128)}, u32[]{:S(2)}) copy-start(f32[4,33]{1,0:T(4,128)} %param.28) | copy-start | bytes 1588
  12.0 9.6 %copy-start.14 = (s32[128]{0:T(128)S(1)}, s32[128]{0:T(128)}, u32[]{:S(2)}) copy-start(s32[128]{0:T(128)} %param.22) | copy-start | bytes 1540
  12.0 63.8 %copy-start.15 = (bf16[1024,512]{1,0:T(8,128)(2,1)S(1)}, bf16[1024,512]{1,0:T(8,128)(2,1)}, u32[]{:S(2)}) copy-start(bf16[1024,512]{1,0:T(8,128)(2,1)} %param.25) | copy-start | bytes 3145732
  12.0 63.8 %all-to-all-start = ((bf16[16,1,128,1024]{3,2,1,0:T(8,128)(2,1)}), bf16[16,1,128,1024]{3,2,1,0:T(8,128)(2,1)}, u32[]{:S(2)}, u32[]{:S(2)}) async-start(bf16[16,1,128,1024]{3,2,1,0:T(8,128)(2,1)} %stack.8), calls=%async_computation | async-start | bytes 8388608 | tf_op jit(solution)/shard_map/all_to_all | solution.py:54
  20.3 182.0 %reduce-scatter.4.cloned.1.call-start = ((), (), s32[]{:S(2)}) async-start(), calls=%async_computation.8 | async-start | bytes 4456448 | tf_op jit(solution)/shard_map/reduce_scatter | solution.py:59
  84.2 6.3 %copy-start.16 = (bf16[1024,512]{1,0:T(8,128)(2,1)S(1)}, bf16[1024,512]{1,0:T(8,128)(2,1)}, u32[]{:S(2)}) copy-start(bf16[1024,512]{1,0:T(8,128)(2,1)} %param.26) | copy-start | bytes 3145732
  107.5 1.8 copy-start.4
  114.5 87.9 %copy-start.2 = (bf16[1,128,1024]{2,1,0:T(8,128)(2,1)S(1)}, bf16[1,128,1024]{2,1,0:T(8,128)(2,1)}, u32[]{:S(2)}) copy-start(bf16[1,128,1024]{2,1,0:T(8,128)(2,1)} %param.21) | copy-start | bytes 786436
  114.5 89.0 %copy-start.10 = (f32[1024]{0:T(1024)S(1)}, f32[1024]{0:T(1024)}, u32[]{:S(2)}) copy-start(f32[1024]{0:T(1024)} %param.29) | copy-start | bytes 12292
  204.5 0.7 copy-start.8
  205.2 55.8 %copy-start.3 = (bf16[1,64,1024]{2,1,0:T(8,128)(2,1)S(1)}, bf16[1,64,1024]{2,1,0:T(8,128)(2,1)}, u32[]{:S(2)}) copy-start(bf16[1,64,1024]{2,1,0:T(8,128)(2,1)} %param.30) | copy-start | bytes 393220
  262.7 33.0 %all-to-all-start.3 = ((bf16[16,1,64,1024]{3,2,1,0:T(8,128)(2,1)}), bf16[16,1,64,1024]{3,2,1,0:T(8,128)(2,1)S(1)}, u32[]{:S(2)}, u32[]{:S(2)}) async-start(bf16[16,1,64,1024]{3,2,1,0:T(8,128)(2,1)} %stack.10), calls=%async_computation.4 | async-start | bytes 4194304 | tf_op jit(solution)/shard_map/all_to_all | solution.py:54
  271.2 30.9 %copy-start.9 = (bf16[8,1024]{1,0:T(8,128)(2,1)S(1)}, bf16[8,1024]{1,0:T(8,128)(2,1)}, u32[]{:S(2)}) copy-start(bf16[8,1024]{1,0:T(8,128)(2,1)} %param.33) | copy-start | bytes 49156
  271.2 30.9 %copy-start.13 = (s32[16]{0:T(128)S(1)}, s32[16]{0:T(128)}, u32[]{:S(2)}) copy-start(s32[16]{0:T(128)} %param.32) | copy-start | bytes 196
  295.7 64.8 %all-to-all-start.2 = ((bf16[2,8,128,1024]{3,2,0,1:T(8,128)(2,1)}), bf16[2,8,128,1024]{3,2,0,1:T(8,128)(2,1)}, u32[]{:S(2)}, u32[]{:S(2)}) async-start(bf16[2,8,128,1024]{3,2,0,1:T(8,128)(2,1)} %copy.81), calls=%async_computation.3 | async-start | bytes 8388608 | tf_op jit(solution)/shard_map/all_to_all | solution.py:68
  301.2 1.7 copy-start.12
  301.2 164.0 %reduce-scatter.6.cloned.1.call-start = ((), (), s32[]{:S(2)}) async-start(), calls=%async_computation.9 | async-start | bytes 2228224 | tf_op jit(solution)/shard_map/reduce_scatter | solution.py:59
  302.9 1.2 copy-start.17
  305.4 55.1 %copy-start.18 = (bf16[1024,512]{1,0:T(8,128)(2,1)S(1)}, bf16[1024,512]{1,0:T(8,128)(2,1)}, u32[]{:S(2)}) copy-start(bf16[1024,512]{1,0:T(8,128)(2,1)} %param.36) | copy-start | bytes 3145732
  360.6 5.9 %copy-start.19 = (bf16[1024,512]{1,0:T(8,128)(2,1)S(1)}, bf16[1024,512]{1,0:T(8,128)(2,1)}, u32[]{:S(2)}) copy-start(bf16[1024,512]{1,0:T(8,128)(2,1)} %param.37) | copy-start | bytes 3145732
  377.2 1.3 copy-start.6
  378.5 1.6 copy-start.5
  380.1 9.9 %copy-start.20 = (bf16[512,1024]{1,0:T(8,128)(2,1)S(1)}, bf16[512,1024]{1,0:T(8,128)(2,1)}, u32[]{:S(2)}) copy-start(bf16[512,1024]{1,0:T(8,128)(2,1)} %param.38) | copy-start | bytes 3145732
  393.8 72.5 %copy-start.11 = (f32[1024]{0:T(1024)S(1)}, f32[1024]{0:T(1024)}, u32[]{:S(2)}) copy-start(f32[1024]{0:T(1024)} %param.39) | copy-start | bytes 12292
  393.8 189.6 %reduce-scatter.8.cloned.1.call-start = ((), (), s32[]{:S(2)}) async-start(), calls=%async_computation.10 | async-start | bytes 2228224 | tf_op jit(solution)/shard_map/reduce_scatter | solution.py:59
  501.3 83.8 %copy-start.1 = (bf16[512,1024]{1,0:T(8,128)(2,1)S(1)}, bf16[512,1024]{1,0:T(8,128)(2,1)}, u32[]{:S(2)}) copy-start(bf16[512,1024]{1,0:T(8,128)(2,1)} %param.27) | copy-start | bytes 3145732
  515.0 68.4 %copy-start.7 = (bf16[1,64,1024]{2,1,0:T(8,128)(2,1)S(1)}, bf16[1,64,1024]{2,1,0:T(8,128)(2,1)}, u32[]{:S(2)}) copy-start(bf16[1,64,1024]{2,1,0:T(8,128)(2,1)} %reduce-scatter.6.cloned.1.call-done) | copy-start | bytes 393220
Sparse Core Ops, SparseCore 0:
  114.6 87.6 reduce-scatter.3
  393.9 71.2 reduce-scatter.5
  515.1 68.2 reduce-scatter.7
